TPU v7x, 32 devices: a whole 2x2x4 slice. The times are simulated.
32 devices in a mesh: row: 8 (over z, x), col: 4 (over y, core).
Axes of the slice: x: 2, y: 2, z: 4, core: 2. Of those that a mesh axis runs over, the one named last changes fastest.
Arguments:
- panels_t: float32 [1024, 2048], P('col', 'row'), as said below
- trailing_t: float32 [3072, 2048], P('col', 'row'), may hold values from -0.125 to 0.125
Outputs:
- r_factor: float32 [1024, 1024], P('row', 'col')
- coefficients: float32 [1024, 3072], P('row', 'col')
Inputs may be any that keep to these rules, and one draw needn't show every extreme that they name: `panels_t`: panel_matrix has full column rank.
All inputs are finite; a program needn't handle non-finite values.
Results may differ from a plain program's by a relative error of at most 0.0003.
Values sent between devices are 32-bit elements; how exact they have to be, the bound alone decides.
A program may use at most 64 MiB of HBM per device.

v0:
```python
import jax
import jax.numpy as jnp
from jax import lax
from jax.experimental import pallas as pl
from jax.experimental.pallas import tpu as pltpu
from jax.sharding import PartitionSpec as P

BLOCK = 128
MICRO = 8
MESH = pl.DeviceIdType.MESH


def product(left, right):
    return jnp.dot(left, right, precision=lax.Precision.HIGHEST)


def contract(left, right, left_dim, right_dim):
    return lax.dot_general(
        left,
        right,
        (((left_dim,), (right_dim,)), ((), ())),
        precision=lax.Precision.HIGHEST,
        preferred_element_type=jnp.float32,
    )


def lanes(tile, lane):
    return jnp.broadcast_to(tile[:, lane : lane + 1], tile.shape)


def sublanes(tile, row):
    return jnp.broadcast_to(tile[row : row + 1, :], tile.shape)


def factor_block(square):
    count = BLOCK // MICRO
    shape = (MICRO, BLOCK)
    row_id = lax.broadcasted_iota(jnp.int32, shape, 0)
    lane_id = lax.broadcasted_iota(jnp.int32, shape, 1)
    rest = [square[MICRO * i : MICRO * (i + 1), :] for i in range(count)]
    unit = [jnp.where(row_id + MICRO * i == lane_id, 1.0, 0.0) for i in range(count)]
    upper, inverse = [], []
    for b in range(count):
        base = MICRO * b
        tile, side = rest[b], unit[b]
        cols = [lanes(tile, base + c) for c in range(MICRO)]
        scales, pivots, rows, sides = [], {}, [], []
        upper_tile, side_tile = jnp.zeros(shape, jnp.float32), jnp.zeros(shape, jnp.float32)
        for k in range(MICRO):
            scale = lax.rsqrt(sublanes(cols[k], k))
            below = cols[k] * scale
            row = sublanes(tile, k) * scale
            side_row = sublanes(side, k) * scale
            for c in range(k + 1, MICRO):
                pivots[c, k] = sublanes(below, c)
                cols[c] = cols[c] - below * pivots[c, k]
            tile = tile - below * row
            side = side - below * side_row
            upper_tile = jnp.where(row_id == k, row, upper_tile)
            side_tile = jnp.where(row_id == k, side_row, side_tile)
            scales.append(scale)
            rows.append(row)
            sides.append(side_row)
        upper.append(jnp.where(row_id + base <= lane_id, upper_tile, 0.0))
        inverse.append(jnp.where(row_id + base >= lane_id, side_tile, 0.0))
        for i in range(b + 1, count):
            tile, side = rest[i], unit[i]
            cols = [lanes(tile, base + c) for c in range(MICRO)]
            for k in range(MICRO):
                below = cols[k] * scales[k]
                for c in range(k + 1, MICRO):
                    cols[c] = cols[c] - below * pivots[c, k]
                tile = tile - below * rows[k]
                side = side - below * sides[k]
            rest[i], unit[i] = tile, side
    return jnp.concatenate(upper, axis=0), jnp.concatenate(inverse, axis=0)


def unstack(stacked_ref, work_ref, width):
    count = stacked_ref.shape[0]

    def block(i, step):
        return stacked_ref[i, :, :, pl.ds(step * width, width)].reshape(width, width)

    for i in range(count):
        for j in range(i, count):
            held = block(i, j - i) if j - i <= count // 2 else block(j, count + i - j).T
            work_ref[pl.ds(i * width, width), pl.ds(j * width, width)] = held
            if j > i:
                work_ref[pl.ds(j * width, width), pl.ds(i * width, width)] = jnp.zeros((width, width), jnp.float32)


def factor_loop(upper_ref, inverse_ref, work_ref, beside):
    total = work_ref.shape[0]
    column = lax.broadcasted_iota(jnp.int32, (BLOCK, total), 1)

    @pl.loop(0, total // BLOCK)
    def _(k):
        beside(k)
        start = pl.multiple_of(k * BLOCK, BLOCK)
        here = pl.ds(start, BLOCK)
        diagonal, inverse = factor_block(work_ref[here, here])
        panel = product(inverse, work_ref[here, :])
        work_ref[here, :] = panel
        work_ref[here, here] = inverse
        upper_ref[here, :] = jnp.where(column >= start + BLOCK, panel, 0.0)
        upper_ref[here, here] = diagonal
        inverse_ref[here, :] = jnp.where(column < start, panel, 0.0)
        inverse_ref[here, here] = inverse

        @pl.loop(k + 1, total // BLOCK)
        def _(i):
            there = pl.ds(pl.multiple_of(i * BLOCK, BLOCK), BLOCK)
            work_ref[there, here] = jnp.zeros((BLOCK, BLOCK), jnp.float32)
            work_ref[there, :] -= contract(work_ref[here, there], work_ref[here, :], 0, 0)


def factor_kernel(gram_ref, upper_ref, inverse_ref, work_ref):
    work_ref[...] = gram_ref[...]
    factor_loop(upper_ref, inverse_ref, work_ref, lambda k: None)


def factor(gram):
    total = gram.shape[0]
    whole = jax.ShapeDtypeStruct((total, total), jnp.float32)
    return pl.pallas_call(
        factor_kernel,
        out_shape=(whole, whole),
        in_specs=[pl.BlockSpec(memory_space=pltpu.VMEM)],
        out_specs=(pl.BlockSpec(memory_space=pltpu.VMEM),) * 2,
        scratch_shapes=[pltpu.VMEM((total, total), jnp.float32)],
        compiler_params=pltpu.CompilerParams(vmem_limit_bytes=32 * 1024 * 1024),
        cost_estimate=pl.CostEstimate(flops=60 * total**3, bytes_accessed=12 * total**2, transcendentals=0),
    )(gram)


def remote(source, target, send, receive, row, col):
    return pltpu.make_async_remote_copy(
        src_ref=source,
        dst_ref=target,
        send_sem=send,
        recv_sem=receive,
        device_id=(row, col),
        device_id_type=MESH,
    )


def greet(peers):
    barrier = pltpu.get_barrier_semaphore()
    for row, col in peers:
        pl.semaphore_signal(barrier, inc=1, device_id=(row, col), device_id_type=MESH)
    pl.semaphore_wait(barrier, len(peers))


def column_peers(cols):
    row, col = lax.axis_index("row"), lax.axis_index("col")
    mate = col + 1 - 2 * lax.rem(col, 2)
    return [(row, lax.rem(col + 2 * t, cols)) for t in range(1, cols // 2)] + [(row, mate)]


def gather_columns(cols, pieces, ready, view, sems):
    line_send, line_recv, mate_send, mate_recv = sems
    row, col = lax.axis_index("row"), lax.axis_index("col")
    mate = col + 1 - 2 * lax.rem(col, 2)
    half = cols // 2
    sent = []

    def launch(copy):
        copy.start()
        sent.append(copy)

    def to_mate(source, owner, s, t):
        launch(remote(source, view(owner, s), mate_send.at[s, t], mate_recv.at[s, t], row, mate))

    def relay(s):
        for t in range(1, half):
            owner = lax.rem(col - 2 * t + cols, cols)
            place = view(owner, s)
            remote(place, place, line_send.at[s, t], line_recv.at[s, t], row, mate).wait_recv()
            to_mate(place, owner, s, t)

    for s in range(pieces):
        source = ready(s)
        for t in range(1, half):
            peer = lax.rem(col + 2 * t, cols)
            launch(remote(source, view(col, s), line_send.at[s, t], line_recv.at[s, t], row, peer))
        to_mate(source, col, s, 0)
        if s > 0:
            relay(s - 1)
    relay(pieces - 1)
    for s in range(pieces):
        for t in range(half):
            place = view(lax.rem(mate - 2 * t + cols, cols), s)
            remote(place, place, mate_send.at[s, t], mate_recv.at[s, t], row, mate).wait_recv()
    for copy in sent:
        copy.wait_send()


def column_sems(cols, pieces):
    return [pltpu.SemaphoreType.DMA((pieces, cols // 2))] * 4


def gather_panel(cols, block_ref, panel_ref, sems):
    pieces = sems[0].shape[0]
    size = block_ref.shape[0] // pieces

    def part(s):
        return pl.ds(s * size, size)

    gather_columns(cols, pieces, lambda s: block_ref.at[part(s)], lambda c, s: panel_ref.at[c, part(s)], sems)
    panel_ref[lax.axis_index("col")] = block_ref[...]


class Reduction:
    def __init__(self, rows, buffer_ref, pair_ref, line_ref, pairs, lines):
        self.buffer, self.pair, self.line = buffer_ref, pair_ref, line_ref
        self.pairs, self.lines = pairs, lines
        self.row, self.col = lax.axis_index("row"), lax.axis_index("col")
        self.half = rows // 2
        self.place, self.side = self.row // 2, lax.rem(self.row, 2)

    def target(self, s, which):
        return 2 * lax.rem(self.place + s, self.half) + which

    def pair_copy(self, s):
        mate = 2 * self.place + 1 - self.side
        source = self.buffer.at[self.target(s, 1 - self.side)]
        return remote(source, self.pair.at[s], self.pairs[0].at[s], self.pairs[1].at[s], mate, self.col)

    def line_copy(self, s):
        owner = self.target(s, self.side)
        source = self.buffer.at[owner]
        return remote(source, self.line.at[s], self.lines[0].at[s], self.lines[1].at[s], owner, self.col)

    def start(self):
        for s in list(range(1, self.half)) + [0]:
            self.pair_copy(s).start()

    def fold(self, s):
        self.pair_copy(s).wait_recv()
        self.buffer[self.target(s, self.side)] += self.pair[s]
        if s > 0:
            self.line_copy(s).start()

    def finish(self):
        self.fold(0)
        total = self.buffer[self.row]
        for s in range(1, self.half):
            self.line_copy(s).wait_recv()
            total = total + self.line[s]
        return total

    def drain(self):
        for s in range(self.half):
            self.pair_copy(s).wait_send()
            if s > 0:
                self.line_copy(s).wait_send()


def reduce_gram(rows, cols, reduction, out_ref, gathers, column, between):
    row, col = lax.axis_index("row"), lax.axis_index("col")
    row_send, row_recv = gathers
    reduction.start()
    for s in range(1, rows // 2):
        reduction.fold(s)
    between()
    sent = []
    total = reduction.finish()
    out_ref[col, row] = total

    def view(c, s):
        return out_ref.at[c, lax.rem(row - s + rows, rows)]

    for s in range(1, rows):
        peer = lax.rem(row + s, rows)
        copy = remote(view(col, 0), view(col, 0), row_send.at[s], row_recv.at[s], peer, col)
        copy.start()
        sent.append(copy)

    def ready(s):
        if s > 0:
            place = view(col, s)
            remote(place, place, row_send.at[s], row_recv.at[s], lax.rem(row + s, rows), col).wait_recv()
        return view(col, s)

    gather_columns(cols, rows, ready, view, column)
    for copy in sent:
        copy.wait_send()
    reduction.drain()


def solve(cross_ref, inverse_ref, middle_ref, slab_ref):
    total = inverse_ref.shape[0]
    step = 2 * BLOCK
    for j in range(0, total, step):
        stop = j + step
        middle_ref[:, j:stop] = contract(cross_ref[:, :stop], inverse_ref[j:stop, :stop], 1, 1)
    wide = total // slab_ref.shape[0]
    for j in range(0, total, step):
        found = contract(middle_ref[:, j:], inverse_ref[j:, j : j + step], 1, 0)
        for t in range(0, step, wide):
            slab_ref[(j + t) // wide] = found[:, t : t + wide]


def spread_slab(rows, slab_ref, out_ref, send, receive):
    row, col = lax.axis_index("row"), lax.axis_index("col")
    sent = []
    for s in range(1, rows):
        peer = lax.rem(row + s, rows)
        copy = remote(slab_ref.at[peer], out_ref.at[row], send.at[s], receive.at[s], peer, col)
        copy.start()
        sent.append(copy)
    out_ref[row] = slab_ref[row]
    for s in range(1, rows):
        place = out_ref.at[lax.rem(row - s + rows, rows)]
        remote(place, place, send.at[s], receive.at[s], lax.rem(row + s, rows), col).wait_recv()
    for copy in sent:
        copy.wait_send()


def main_kernel(rows, cols, width, *refs):
    block_ref, trailing_ref, upper_out, coef_out = refs[:4]
    panel_ref, part_ref, near_pair_ref, near_line_ref, stacked_ref = refs[4:9]
    cross_ref, pair_ref, line_ref, work_ref, upper_ref, inverse_ref, summed_ref, middle_ref, slab_ref = refs[9:18]
    gathers, spreads, near_pairs, near_lines, pairs, lines = (refs[18 + 2 * i : 20 + 2 * i] for i in range(6))
    first, column = refs[30:34], refs[34:38]
    row, col = lax.axis_index("row"), lax.axis_index("col")
    greet([(lax.rem(row + s, rows), col) for s in range(1, rows)] + column_peers(cols))
    gather_panel(cols, block_ref, panel_ref, first)
    for step in range(cols // 2 + 1):
        held = contract(block_ref[...], panel_ref[lax.rem(col + step, cols)], 1, 1)
        part_ref[:, :, step * width : (step + 1) * width] = held.reshape(rows, width // rows, width)

    def multiply():
        panel = panel_ref[...].reshape(width * cols, panel_ref.shape[2])

        @pl.loop(0, rows)
        def _(r):
            cross_ref[r] = contract(trailing_ref[r], panel, 1, 1)

    near = Reduction(rows, part_ref, near_pair_ref, near_line_ref, near_pairs, near_lines)
    reduce_gram(rows, cols, near, stacked_ref, gathers, column, multiply)
    wide = Reduction(rows, cross_ref, pair_ref, line_ref, pairs, lines)
    wide.start()
    unstack(stacked_ref, work_ref, width)

    def beside(k):
        for s in range(1, rows // 2):
            pl.when(k == s + 1)(lambda s=s: wide.fold(s))

    factor_loop(upper_ref, inverse_ref, work_ref, beside)
    upper_out[...] = upper_ref[
        pl.ds(pl.multiple_of(row * upper_out.shape[0], MICRO), upper_out.shape[0]),
        pl.ds(pl.multiple_of(col * upper_out.shape[1], BLOCK), upper_out.shape[1]),
    ]
    summed_ref[...] = wide.finish()
    solve(summed_ref, inverse_ref, middle_ref, slab_ref)
    spread_slab(rows, slab_ref, coef_out, *spreads)
    wide.drain()


def direct(panels_t, trailing_t, rows, cols):
    width, depth = panels_t.shape
    total = width * cols
    half = rows // 2
    trailing = trailing_t.reshape(rows, -1, depth)
    thick = trailing.shape[1]
    near = (width // rows, (cols // 2 + 1) * width)
    vmem = pl.BlockSpec(memory_space=pltpu.VMEM)
    shapes = [
        (cols, width, depth),
        (rows,) + near,
        (half,) + near,
        (half,) + near,
        (cols, rows) + near,
        (rows, thick, total),
        (half, thick, total),
        (half, thick, total),
        (total, total),
        (total, total),
        (total, total),
        (thick, total),
        (thick, total),
        (rows, thick, total // rows),
    ]
    semaphores = [pltpu.SemaphoreType.DMA((rows,))] * 4 + [pltpu.SemaphoreType.DMA((half,))] * 8
    r_block, spread = pl.pallas_call(
        lambda *refs: main_kernel(rows, cols, width, *refs),
        out_shape=(
            jax.ShapeDtypeStruct((total // rows, total // cols), jnp.float32),
            jax.ShapeDtypeStruct((rows, thick, total // rows), jnp.float32),
        ),
        in_specs=[vmem] * 2,
        out_specs=(vmem, vmem),
        scratch_shapes=[pltpu.VMEM(shape, jnp.float32) for shape in shapes]
        + semaphores
        + column_sems(cols, 2)
        + column_sems(cols, rows),
        compiler_params=pltpu.CompilerParams(collective_id=1, has_side_effects=True, vmem_limit_bytes=48 * 1024 * 1024),
    )(panels_t, trailing)
    return r_block, spread.transpose(2, 0, 1).reshape(total // rows, -1)


def plain(panels_t, trailing_t):
    panel = lax.all_gather(panels_t, "col", axis=0, tiled=True)
    gram_part = lax.psum_scatter(product(panels_t, panel.T), "row", scatter_dimension=0, tiled=True)
    gram = lax.all_gather(gram_part, ("col", "row"), axis=0, tiled=True)
    cross = lax.psum_scatter(product(trailing_t, panel.T), "row", scatter_dimension=0, tiled=True)
    r_full, invert = factor(gram)
    slab = product(product(cross, invert.T), invert)
    return r_full, lax.all_to_all(slab, "row", split_axis=1, concat_axis=0, tiled=True).T


def local(panels_t, trailing_t):
    rows, cols = lax.axis_size("row"), lax.axis_size("col")
    width = panels_t.shape[0]
    total = width * cols
    thick = trailing_t.shape[0] // rows
    tiled = width % BLOCK == 0 and total // rows % BLOCK == 0 and width // rows % MICRO == 0 and thick % MICRO == 0
    if tiled and rows % 2 == 0 and cols % 2 == 0 and rows // 2 < total // BLOCK:
        return direct(panels_t, trailing_t, rows, cols)
    r_full, coef_block = plain(panels_t, trailing_t)
    rows_out = total // rows
    row_start = lax.axis_index("row") * rows_out
    col_start = lax.axis_index("col") * width
    r_block = lax.dynamic_slice(r_full, (row_start, col_start), (rows_out, width))
    return (r_block, coef_block)


def solution(mesh):
    placed = (P("col", "row"), P("col", "row"))
    return jax.shard_map(
        local,
        mesh=mesh,
        in_specs=placed,
        out_specs=(P("row", "col"), P("row", "col")),
        check_vma=False,
    )
```

profile of v0, /device:TPU:0, one launch (start us, length us, event | category | flops | bytes accessed | tf_op | source)
XLA Modules:
  0.0 133.5 jit_solution(9306427291521040020)
XLA Ops:
  0.6 0.0 copy-start
  0.6 1.1 copy-done
  1.8 0.0 copy-start.1
  1.8 0.9 copy-done.1
  2.7 129.2 %shard_map.41 = (f32[128,256]{1,0:T(8,128)S(1)}, f32[8,96,128]{2,1,0:T(8,128)S(1)}) custom-call(f32[256,256]{1,0:T(8,128)S(1)} %copy-done.1, f32[8,96,256]{2,1,0:T(8,128)S(1)} %bitcast.4), custom_call_target="tpu_custom_call" | custom-call | tf_op jit(solution)/shard_map/pallas_call | solution.py:387
  131.9 0.9 copy.4
  132.8 0.7 copy.6
Async XLA Ops:
  0.6 1.1 copy-start
  1.8 0.9 copy-start.1
where the time goes:
time: 134 us
  Pallas kernels  129 us (96%)
  local copies, waits for them, and re-layouts  3.65 us (3%)
    pallas_call x1, Pallas kernels, direct(): pl.pallas_call(lambda *refs: main_kernel(rows, cols, width, *refs), out_s...  129 us
    unnamed x6, local copies, waits for them, and re-layouts  3.65 us

commit v1 on v0

--- a/solution.py
+++ b/solution.py
@@ -7,6 +7,7 @@
 
 BLOCK = 128
 MICRO = 8
+LATE = 1
 MESH = pl.DeviceIdType.MESH
 
 
@@ -39,11 +40,11 @@
     lane_id = lax.broadcasted_iota(jnp.int32, shape, 1)
     rest = [square[MICRO * i : MICRO * (i + 1), :] for i in range(count)]
     unit = [jnp.where(row_id + MICRO * i == lane_id, 1.0, 0.0) for i in range(count)]
+    cols = [lanes(rest[0], c) for c in range(MICRO)]
     upper, inverse = [], []
     for b in range(count):
         base = MICRO * b
         tile, side = rest[b], unit[b]
-        cols = [lanes(tile, base + c) for c in range(MICRO)]
         scales, pivots, rows, sides = [], {}, [], []
         upper_tile, side_tile = jnp.zeros(shape, jnp.float32), jnp.zeros(shape, jnp.float32)
         for k in range(MICRO):
@@ -63,31 +64,23 @@
             sides.append(side_row)
         upper.append(jnp.where(row_id + base <= lane_id, upper_tile, 0.0))
         inverse.append(jnp.where(row_id + base >= lane_id, side_tile, 0.0))
+        following = []
         for i in range(b + 1, count):
             tile, side = rest[i], unit[i]
             cols = [lanes(tile, base + c) for c in range(MICRO)]
+            ahead = [lanes(tile, base + MICRO + c) for c in range(MICRO)] if i == b + 1 else []
             for k in range(MICRO):
                 below = cols[k] * scales[k]
                 for c in range(k + 1, MICRO):
                     cols[c] = cols[c] - below * pivots[c, k]
+                for c in range(len(ahead)):
+                    ahead[c] = ahead[c] - below * sublanes(below, c)
                 tile = tile - below * rows[k]
                 side = side - below * sides[k]
             rest[i], unit[i] = tile, side
+            following = ahead or following
+        cols = following
     return jnp.concatenate(upper, axis=0), jnp.concatenate(inverse, axis=0)
-
-
-def unstack(stacked_ref, work_ref, width):
-    count = stacked_ref.shape[0]
-
-    def block(i, step):
-        return stacked_ref[i, :, :, pl.ds(step * width, width)].reshape(width, width)
-
-    for i in range(count):
-        for j in range(i, count):
-            held = block(i, j - i) if j - i <= count // 2 else block(j, count + i - j).T
-            work_ref[pl.ds(i * width, width), pl.ds(j * width, width)] = held
-            if j > i:
-                work_ref[pl.ds(j * width, width), pl.ds(i * width, width)] = jnp.zeros((width, width), jnp.float32)
 
 
 def factor_loop(upper_ref, inverse_ref, work_ref, beside):
@@ -96,10 +89,10 @@
 
     @pl.loop(0, total // BLOCK)
     def _(k):
-        beside(k)
         start = pl.multiple_of(k * BLOCK, BLOCK)
         here = pl.ds(start, BLOCK)
         diagonal, inverse = factor_block(work_ref[here, here])
+        beside(k)
         panel = product(inverse, work_ref[here, :])
         work_ref[here, :] = panel
         work_ref[here, here] = inverse
@@ -257,36 +250,108 @@
                 self.line_copy(s).wait_send()
 
 
-def reduce_gram(rows, cols, reduction, out_ref, gathers, column, between):
-    row, col = lax.axis_index("row"), lax.axis_index("col")
-    row_send, row_recv = gathers
-    reduction.start()
-    for s in range(1, rows // 2):
-        reduction.fold(s)
-    between()
-    sent = []
-    total = reduction.finish()
-    out_ref[col, row] = total
-
-    def view(c, s):
-        return out_ref.at[c, lax.rem(row - s + rows, rows)]
-
-    for s in range(1, rows):
-        peer = lax.rem(row + s, rows)
-        copy = remote(view(col, 0), view(col, 0), row_send.at[s], row_recv.at[s], peer, col)
+class Gram:
+    STAGES = 7
+
+    def __init__(self, rows, cols, width, panel_ref, buffers, sems):
+        self.rows, self.cols, self.width, self.panel = rows, cols, width, panel_ref
+        self.buffers, self.sems = buffers, sems
+        self.row, self.col = lax.axis_index("row"), lax.axis_index("col")
+        self.half, self.across = rows // 2, cols // 2
+        self.place, self.side = self.row // 2, lax.rem(self.row, 2)
+        self.beside = 2 * self.place + 1 - self.side
+        self.mate = self.col + 1 - 2 * lax.rem(self.col, 2)
+        self.chunks = gram_chunks(cols)
+
+    def put(self, source, target, which, ch, n, row, col):
+        send, receive = self.sems[which]
+        copy = remote(source, target, send.at[ch, n], receive.at[ch, n], row, col)
         copy.start()
-        sent.append(copy)
-
-    def ready(s):
-        if s > 0:
-            place = view(col, s)
-            remote(place, place, row_send.at[s], row_recv.at[s], lax.rem(row + s, rows), col).wait_recv()
-        return view(col, s)
-
-    gather_columns(cols, rows, ready, view, column)
-    for copy in sent:
-        copy.wait_send()
-    reduction.drain()
+
+    def got(self, place, which, ch, n):
+        send, receive = self.sems[which]
+        remote(place, place, send.at[ch, n], receive.at[ch, n], self.beside, self.col).wait_recv()
+
+    def peer(self, s):
+        return lax.rem(self.place + s, self.half)
+
+    def stage(self, ch, st):
+        own, first, last = self.chunks[ch]
+        part, pair, line, full = self.buffers[ch]
+        side, col = self.side, self.col
+        thin = self.width // (self.rows * self.cols)
+        if st == 0:
+            strip = self.panel[own, pl.ds(pl.multiple_of(col * (thin * self.rows), MICRO), thin * self.rows), :]
+            right = self.panel[first:last].reshape((last - first) * self.width, -1)
+            held = contract(strip, right, 1, 1)
+            for r in range(self.rows):
+                part[r % 2, r // 2] = held[r * thin : (r + 1) * thin]
+            self.put(part.at[1 - side], pair, 0, ch, 0, self.beside, col)
+        if st == 1:
+            self.got(pair, 0, ch, 0)
+            for s in range(self.half):
+                part[side, s] += pair[s]
+            for s in range(1, self.half):
+                to = self.peer(s)
+                self.put(part.at[side, to], line.at[s], 1, ch, s, 2 * to + side, col)
+        if st == 2:
+            total = part[side, self.place]
+            for s in range(1, self.half):
+                self.got(line.at[s], 1, ch, s)
+                total = total + line[s]
+            mine = full.at[col, side, self.place]
+            full[col, side, self.place] = total
+            for s in range(1, self.half):
+                self.put(mine, mine, 2, ch, s, 2 * self.peer(s) + side, col)
+        if st == 3:
+            for s in range(1, self.half):
+                self.got(full.at[col, side, self.peer(self.half - s)], 2, ch, s)
+            mine = full.at[col, side]
+            self.put(mine, mine, 3, ch, 0, self.beside, col)
+        if st == 4:
+            self.got(full.at[col, 1 - side], 3, ch, 0)
+            mine = full.at[col]
+            for t in range(1, self.across):
+                self.put(mine, mine, 4, ch, t, self.row, lax.rem(col + 2 * t, self.cols))
+            self.put(mine, mine, 5, ch, 0, self.row, self.mate)
+        if st == 5:
+            for t in range(1, self.across):
+                place = full.at[lax.rem(col - 2 * t + self.cols, self.cols)]
+                self.got(place, 4, ch, t)
+                self.put(place, place, 5, ch, t, self.row, self.mate)
+        if st == 6:
+            for t in range(self.across):
+                self.got(full.at[lax.rem(self.mate - 2 * t + self.cols, self.cols)], 5, ch, t)
+
+    def wave(self, w):
+        for ch in range(len(self.chunks)):
+            if 0 <= w - ch < self.STAGES:
+                self.stage(ch, w - ch)
+
+    def place_chunk(self, ch, work_ref, add):
+        own, first, last = self.chunks[ch]
+        full = self.buffers[ch][3]
+        thin = self.width // (self.rows * self.cols)
+        columns = pl.ds(first * self.width, (last - first) * self.width)
+        for c in range(self.cols):
+            for r in range(self.rows):
+                there = pl.ds(own * self.width + (c * self.rows + r) * thin, thin)
+                held = full[c, r % 2, r // 2]
+                work_ref[there, columns] = work_ref[there, columns] + held if add else held
+
+    def drain(self):
+        for ch, (part, pair, line, full) in enumerate(self.buffers):
+            one, all_places, strip = full.at[0, 0, 0], full.at[0, 0], full.at[0]
+            steps = [(0, 0, pair)] + [(1, s, one) for s in range(1, self.half)] + [(2, s, one) for s in range(1, self.half)]
+            steps += [(3, 0, all_places)] + [(4, t, strip) for t in range(1, self.across)]
+            steps += [(5, t, strip) for t in range(self.across)]
+            for which, n, place in steps:
+                send, receive = self.sems[which]
+                remote(place, place, send.at[ch, n], receive.at[ch, n], self.beside, self.col).wait_send()
+
+
+def gram_chunks(cols):
+    return [(0, 0, 1), (0, 1, cols)] + [(q, q, cols) for q in range(1, cols)]
 
 
 def solve(cross_ref, inverse_ref, middle_ref, slab_ref):
@@ -319,34 +384,50 @@
 
 
 def main_kernel(rows, cols, width, *refs):
-    block_ref, trailing_ref, upper_out, coef_out = refs[:4]
-    panel_ref, part_ref, near_pair_ref, near_line_ref, stacked_ref = refs[4:9]
-    cross_ref, pair_ref, line_ref, work_ref, upper_ref, inverse_ref, summed_ref, middle_ref, slab_ref = refs[9:18]
-    gathers, spreads, near_pairs, near_lines, pairs, lines = (refs[18 + 2 * i : 20 + 2 * i] for i in range(6))
-    first, column = refs[30:34], refs[34:38]
+    block_ref, trailing_ref, upper_out, coef_out, panel_ref = refs[:5]
+    cross_ref, pair_ref, line_ref, work_ref, upper_ref, inverse_ref, summed_ref, middle_ref, slab_ref = refs[5:14]
+    spreads, pairs, lines = (refs[14 + 2 * i : 16 + 2 * i] for i in range(3))
+    first = refs[20:24]
+    steps = [refs[24 + 2 * i : 26 + 2 * i] for i in range(6)]
+    chunks = gram_chunks(cols)
+    buffers = [refs[36 + 4 * i : 40 + 4 * i] for i in range(len(chunks))]
     row, col = lax.axis_index("row"), lax.axis_index("col")
     greet([(lax.rem(row + s, rows), col) for s in range(1, rows)] + column_peers(cols))
     gather_panel(cols, block_ref, panel_ref, first)
-    for step in range(cols // 2 + 1):
-        held = contract(block_ref[...], panel_ref[lax.rem(col + step, cols)], 1, 1)
-        part_ref[:, :, step * width : (step + 1) * width] = held.reshape(rows, width // rows, width)
-
-    def multiply():
+    gram = Gram(rows, cols, width, panel_ref, buffers, steps)
+    wide = Reduction(rows, cross_ref, pair_ref, line_ref, pairs, lines)
+    total = work_ref.shape[0]
+
+    def multiply(begin, end):
         panel = panel_ref[...].reshape(width * cols, panel_ref.shape[2])
 
-        @pl.loop(0, rows)
+        @pl.loop(begin, end)
         def _(r):
             cross_ref[r] = contract(trailing_ref[r], panel, 1, 1)
 
-    near = Reduction(rows, part_ref, near_pair_ref, near_line_ref, near_pairs, near_lines)
-    reduce_gram(rows, cols, near, stacked_ref, gathers, column, multiply)
-    wide = Reduction(rows, cross_ref, pair_ref, line_ref, pairs, lines)
-    wide.start()
-    unstack(stacked_ref, work_ref, width)
+    ready = Gram.STAGES
+    gram.wave(0)
+    gram.wave(1)
+    work_ref[...] = jnp.zeros_like(work_ref)
+    gram.wave(2)
+    multiply(0, rows // 2)
+    gram.wave(3)
+    gram.wave(4)
+    multiply(rows // 2, rows)
+    gram.wave(5)
+    gram.wave(6)
+    gram.place_chunk(0, work_ref, False)
 
     def beside(k):
+        for w in range(ready, ready + len(chunks) - 1):
+            @pl.when(k == w - ready)
+            def _(w=w):
+                gram.wave(w)
+                gram.place_chunk(w - ready + 1, work_ref, w > ready)
+                if w == ready + LATE:
+                    wide.start()
         for s in range(1, rows // 2):
-            pl.when(k == s + 1)(lambda s=s: wide.fold(s))
+            pl.when(k == s + LATE + 1)(lambda s=s: wide.fold(s))
 
     factor_loop(upper_ref, inverse_ref, work_ref, beside)
     upper_out[...] = upper_ref[
@@ -357,6 +438,7 @@
     solve(summed_ref, inverse_ref, middle_ref, slab_ref)
     spread_slab(rows, slab_ref, coef_out, *spreads)
     wide.drain()
+    gram.drain()
 
 
 def direct(panels_t, trailing_t, rows, cols):
@@ -365,14 +447,10 @@
     half = rows // 2
     trailing = trailing_t.reshape(rows, -1, depth)
     thick = trailing.shape[1]
-    near = (width // rows, (cols // 2 + 1) * width)
+    thin = width // (rows * cols)
     vmem = pl.BlockSpec(memory_space=pltpu.VMEM)
     shapes = [
         (cols, width, depth),
-        (rows,) + near,
-        (half,) + near,
-        (half,) + near,
-        (cols, rows) + near,
         (rows, thick, total),
         (half, thick, total),
         (half, thick, total),
@@ -383,7 +461,14 @@
         (thick, total),
         (rows, thick, total // rows),
     ]
-    semaphores = [pltpu.SemaphoreType.DMA((rows,))] * 4 + [pltpu.SemaphoreType.DMA((half,))] * 8
+    chunks = gram_chunks(cols)
+    staged = []
+    for _, begin, end in chunks:
+        wide = (end - begin) * width
+        staged += [(2, half, thin, wide), (half, thin, wide), (half, thin, wide), (cols, 2, half, thin, wide)]
+    semaphores = [pltpu.SemaphoreType.DMA((rows,))] * 2 + [pltpu.SemaphoreType.DMA((half,))] * 4
+    steps = [1, half, half, 1, cols // 2, cols // 2]
+    stepped = [pltpu.SemaphoreType.DMA((len(chunks), n)) for n in steps for _ in range(2)]
     r_block, spread = pl.pallas_call(
         lambda *refs: main_kernel(rows, cols, width, *refs),
         out_shape=(
@@ -395,7 +480,8 @@
         scratch_shapes=[pltpu.VMEM(shape, jnp.float32) for shape in shapes]
         + semaphores
         + column_sems(cols, 2)
-        + column_sems(cols, rows),
+        + stepped
+        + [pltpu.VMEM(shape, jnp.float32) for shape in staged],
         compiler_params=pltpu.CompilerParams(collective_id=1, has_side_effects=True, vmem_limit_bytes=48 * 1024 * 1024),
     )(panels_t, trailing)
     return r_block, spread.transpose(2, 0, 1).reshape(total // rows, -1)
@@ -416,8 +502,8 @@
     width = panels_t.shape[0]
     total = width * cols
     thick = trailing_t.shape[0] // rows
-    tiled = width % BLOCK == 0 and total // rows % BLOCK == 0 and width // rows % MICRO == 0 and thick % MICRO == 0
-    if tiled and rows % 2 == 0 and cols % 2 == 0 and rows // 2 < total // BLOCK:
+    tiled = width % BLOCK == 0 and total // rows % BLOCK == 0 and width // rows % (cols * MICRO) == 0 and thick % MICRO == 0
+    if tiled and rows % 2 == 0 and cols % 2 == 0 and rows // 2 + LATE < total // BLOCK and cols >= 4:
         return direct(panels_t, trailing_t, rows, cols)
     r_full, coef_block = plain(panels_t, trailing_t)
     rows_out = total // rows

time: 134 us -> 121 us (0.903)
  Pallas kernels: 129 us -> 116 us
    pallas_call x1, Pallas kernels: 129 us -> 116 us  [direct(): pl.pallas_call(lambda *refs: main_kernel(rows, cols, width, *refs), out_s...]
where the time goes in v1:
time: 121 us
  Pallas kernels  116 us (96%)
  local copies, waits for them, and re-layouts  3.65 us (3%)
    pallas_call x1, Pallas kernels, direct(): pl.pallas_call(lambda *refs: main_kernel(rows, cols, width, *refs), out_s...  116 us
    unnamed x6, local copies, waits for them, and re-layouts  3.65 us

profile of v1, /device:TPU:0, one launch (start us, length us, event | category | flops | bytes accessed | tf_op | source)
XLA Modules:
  0.0 120.7 jit_solution(3498327444201342521)
XLA Ops:
  0.6 0.0 copy-start
  0.6 1.1 copy-done
  1.8 0.0 copy-start.1
  1.8 0.9 copy-done.1
  2.7 116.5 %shard_map.41 = (f32[128,256]{1,0:T(8,128)S(1)}, f32[8,96,128]{2,1,0:T(8,128)S(1)}) custom-call(f32[256,256]{1,0:T(8,128)S(1)} %copy-done.1, f32[8,96,256]{2,1,0:T(8,128)S(1)} %bitcast.4), custom_call_target="tpu_custom_call" | custom-call | tf_op jit(solution)/shard_map/pallas_call | solution.py:472
  119.2 0.9 copy.4
  120.1 0.7 copy.6
Async XLA Ops:
  0.6 1.1 copy-start
  1.8 0.9 copy-start.1

commit v2 on v1

--- a/solution.py
+++ b/solution.py
@@ -225,9 +225,9 @@
         source = self.buffer.at[owner]
         return remote(source, self.line.at[s], self.lines[0].at[s], self.lines[1].at[s], owner, self.col)
 
-    def start(self):
-        for s in list(range(1, self.half)) + [0]:
-            self.pair_copy(s).start()
+    def start(self, begin, end):
+        for s in range(begin, end):
+            self.pair_copy(s % self.half).start()
 
     def fold(self, s):
         self.pair_copy(s).wait_recv()
@@ -417,6 +417,7 @@
     gram.wave(5)
     gram.wave(6)
     gram.place_chunk(0, work_ref, False)
+    wide.start(1, 3)
 
     def beside(k):
         for w in range(ready, ready + len(chunks) - 1):
@@ -424,10 +425,10 @@
             def _(w=w):
                 gram.wave(w)
                 gram.place_chunk(w - ready + 1, work_ref, w > ready)
-                if w == ready + LATE:
-                    wide.start()
+                if w == ready:
+                    wide.start(3, rows // 2 + 1)
         for s in range(1, rows // 2):
-            pl.when(k == s + LATE + 1)(lambda s=s: wide.fold(s))
+            pl.when(k == s + LATE)(lambda s=s: wide.fold(s))
 
     factor_loop(upper_ref, inverse_ref, work_ref, beside)
     upper_out[...] = upper_ref[
@@ -503,7 +504,7 @@
     total = width * cols
     thick = trailing_t.shape[0] // rows
     tiled = width % BLOCK == 0 and total // rows % BLOCK == 0 and width // rows % (cols * MICRO) == 0 and thick % MICRO == 0
-    if tiled and rows % 2 == 0 and cols % 2 == 0 and rows // 2 + LATE < total // BLOCK and cols >= 4:
+    if tiled and rows % 2 == 0 and cols % 2 == 0 and rows // 2 + LATE < total // BLOCK and cols >= 4 and rows >= 4:
         return direct(panels_t, trailing_t, rows, cols)
     r_full, coef_block = plain(panels_t, trailing_t)
     rows_out = total // rows

time: 121 us -> 121 us (level)
  no operation moved by 1% of the time
where the time goes in v2:
time: 121 us
  Pallas kernels  117 us (97%)
  local copies, waits for them, and re-layouts  3.65 us (3%)
    pallas_call x1, Pallas kernels, direct(): pl.pallas_call(lambda *refs: main_kernel(rows, cols, width, *refs), out_s...  117 us
    unnamed x6, local copies, waits for them, and re-layouts  3.65 us

profile of v2, /device:TPU:0, one launch (start us, length us, event | category | flops | bytes accessed | tf_op | source)
XLA Modules:
  0.0 120.8 jit_solution(14519720057489679272)
XLA Ops:
  0.6 0.0 copy-start
  0.6 1.1 copy-done
  1.8 0.0 copy-start.1
  1.8 0.9 copy-done.1
  2.7 116.5 %shard_map.41 = (f32[128,256]{1,0:T(8,128)S(1)}, f32[8,96,128]{2,1,0:T(8,128)S(1)}) custom-call(f32[256,256]{1,0:T(8,128)S(1)} %copy-done.1, f32[8,96,256]{2,1,0:T(8,128)S(1)} %bitcast.4), custom_call_target="tpu_custom_call" | custom-call | tf_op jit(solution)/shard_map/pallas_call | solution.py:473
  119.2 0.9 copy.4
  120.2 0.7 copy.6
Async XLA Ops:
  0.6 1.1 copy-start
  1.8 0.9 copy-start.1

commit v3 on v2

--- a/solution.py
+++ b/solution.py
@@ -261,7 +261,7 @@
         self.place, self.side = self.row // 2, lax.rem(self.row, 2)
         self.beside = 2 * self.place + 1 - self.side
         self.mate = self.col + 1 - 2 * lax.rem(self.col, 2)
-        self.chunks = gram_chunks(cols)
+        self.chunks = gram_chunks(cols, width // BLOCK)
 
     def put(self, source, target, which, ch, n, row, col):
         send, receive = self.sems[which]
@@ -279,10 +279,14 @@
         own, first, last = self.chunks[ch]
         part, pair, line, full = self.buffers[ch]
         side, col = self.side, self.col
-        thin = self.width // (self.rows * self.cols)
+        thin = part.shape[2]
         if st == 0:
-            strip = self.panel[own, pl.ds(pl.multiple_of(col * (thin * self.rows), MICRO), thin * self.rows), :]
-            right = self.panel[first:last].reshape((last - first) * self.width, -1)
+            if first is None:
+                strip = self.panel[0, own * BLOCK : (own + 1) * BLOCK, :]
+                right = self.panel[col]
+            else:
+                strip = self.panel[own, pl.ds(pl.multiple_of(col * (thin * self.rows), MICRO), thin * self.rows), :]
+                right = self.panel[first:last].reshape((last - first) * self.width, -1)
             held = contract(strip, right, 1, 1)
             for r in range(self.rows):
                 part[r % 2, r // 2] = held[r * thin : (r + 1) * thin]
@@ -331,11 +335,15 @@
     def place_chunk(self, ch, work_ref, add):
         own, first, last = self.chunks[ch]
         full = self.buffers[ch][3]
-        thin = self.width // (self.rows * self.cols)
-        columns = pl.ds(first * self.width, (last - first) * self.width)
+        thin = full.shape[3]
         for c in range(self.cols):
             for r in range(self.rows):
-                there = pl.ds(own * self.width + (c * self.rows + r) * thin, thin)
+                if first is None:
+                    there = pl.ds(own * BLOCK + r * thin, thin)
+                    columns = pl.ds(c * self.width, self.width)
+                else:
+                    there = pl.ds(own * self.width + (c * self.rows + r) * thin, thin)
+                    columns = pl.ds(first * self.width, (last - first) * self.width)
                 held = full[c, r % 2, r // 2]
                 work_ref[there, columns] = work_ref[there, columns] + held if add else held
 
@@ -350,11 +358,19 @@
                 remote(place, place, send.at[ch, n], receive.at[ch, n], self.beside, self.col).wait_send()
 
 
-def gram_chunks(cols):
-    return [(0, 0, 1), (0, 1, cols)] + [(q, q, cols) for q in range(1, cols)]
-
-
-def solve(cross_ref, inverse_ref, middle_ref, slab_ref):
+def gram_chunks(cols, halves):
+    return [(h, None, None) for h in range(halves)] + [(q, q, cols) for q in range(1, cols)]
+
+
+def chunk_shape(chunk, rows, cols, width):
+    _, begin, end = chunk
+    if begin is None:
+        return BLOCK // rows, width
+    return width // (rows * cols), (end - begin) * width
+
+
+def solve(rows, cross_ref, inverse_ref, middle_ref, slab_ref, out_ref, send, receive):
+    row, col = lax.axis_index("row"), lax.axis_index("col")
     total = inverse_ref.shape[0]
     step = 2 * BLOCK
     for j in range(0, total, step):
@@ -364,23 +380,24 @@
     for j in range(0, total, step):
         found = contract(middle_ref[:, j:], inverse_ref[j:, j : j + step], 1, 0)
         for t in range(0, step, wide):
-            slab_ref[(j + t) // wide] = found[:, t : t + wide]
-
-
-def spread_slab(rows, slab_ref, out_ref, send, receive):
+            peer = (j + t) // wide
+            slab_ref[peer] = found[:, t : t + wide]
+
+            @pl.when(row != peer)
+            def _(peer=peer):
+                s = lax.rem(peer - row + rows, rows)
+                remote(slab_ref.at[peer], out_ref.at[row], send.at[s], receive.at[s], peer, col).start()
+
+
+def settle_slab(rows, slab_ref, out_ref, send, receive):
     row, col = lax.axis_index("row"), lax.axis_index("col")
-    sent = []
-    for s in range(1, rows):
-        peer = lax.rem(row + s, rows)
-        copy = remote(slab_ref.at[peer], out_ref.at[row], send.at[s], receive.at[s], peer, col)
-        copy.start()
-        sent.append(copy)
     out_ref[row] = slab_ref[row]
     for s in range(1, rows):
         place = out_ref.at[lax.rem(row - s + rows, rows)]
         remote(place, place, send.at[s], receive.at[s], lax.rem(row + s, rows), col).wait_recv()
-    for copy in sent:
-        copy.wait_send()
+    for s in range(1, rows):
+        place = slab_ref.at[lax.rem(row + s, rows)]
+        remote(place, place, send.at[s], receive.at[s], lax.rem(row + s, rows), col).wait_send()
 
 
 def main_kernel(rows, cols, width, *refs):
@@ -389,7 +406,7 @@
     spreads, pairs, lines = (refs[14 + 2 * i : 16 + 2 * i] for i in range(3))
     first = refs[20:24]
     steps = [refs[24 + 2 * i : 26 + 2 * i] for i in range(6)]
-    chunks = gram_chunks(cols)
+    chunks = gram_chunks(cols, width // BLOCK)
     buffers = [refs[36 + 4 * i : 40 + 4 * i] for i in range(len(chunks))]
     row, col = lax.axis_index("row"), lax.axis_index("col")
     greet([(lax.rem(row + s, rows), col) for s in range(1, rows)] + column_peers(cols))
@@ -407,17 +424,18 @@
 
     ready = Gram.STAGES
     gram.wave(0)
+    work_ref[...] = jnp.zeros_like(work_ref)
     gram.wave(1)
-    work_ref[...] = jnp.zeros_like(work_ref)
+    multiply(0, rows // 4)
     gram.wave(2)
-    multiply(0, rows // 2)
+    multiply(rows // 4, rows // 2)
     gram.wave(3)
+    multiply(rows // 2, 3 * rows // 4)
     gram.wave(4)
-    multiply(rows // 2, rows)
+    multiply(3 * rows // 4, rows)
     gram.wave(5)
     gram.wave(6)
     gram.place_chunk(0, work_ref, False)
-    wide.start(1, 3)
 
     def beside(k):
         for w in range(ready, ready + len(chunks) - 1):
@@ -426,7 +444,7 @@
                 gram.wave(w)
                 gram.place_chunk(w - ready + 1, work_ref, w > ready)
                 if w == ready:
-                    wide.start(3, rows // 2 + 1)
+                    wide.start(1, rows // 2 + 1)
         for s in range(1, rows // 2):
             pl.when(k == s + LATE)(lambda s=s: wide.fold(s))
 
@@ -436,8 +454,8 @@
         pl.ds(pl.multiple_of(col * upper_out.shape[1], BLOCK), upper_out.shape[1]),
     ]
     summed_ref[...] = wide.finish()
-    solve(summed_ref, inverse_ref, middle_ref, slab_ref)
-    spread_slab(rows, slab_ref, coef_out, *spreads)
+    solve(rows, summed_ref, inverse_ref, middle_ref, slab_ref, coef_out, *spreads)
+    settle_slab(rows, slab_ref, coef_out, *spreads)
     wide.drain()
     gram.drain()
 
@@ -448,7 +466,6 @@
     half = rows // 2
     trailing = trailing_t.reshape(rows, -1, depth)
     thick = trailing.shape[1]
-    thin = width // (rows * cols)
     vmem = pl.BlockSpec(memory_space=pltpu.VMEM)
     shapes = [
         (cols, width, depth),
@@ -462,10 +479,10 @@
         (thick, total),
         (rows, thick, total // rows),
     ]
-    chunks = gram_chunks(cols)
+    chunks = gram_chunks(cols, width // BLOCK)
     staged = []
-    for _, begin, end in chunks:
-        wide = (end - begin) * width
+    for chunk in chunks:
+        thin, wide = chunk_shape(chunk, rows, cols, width)
         staged += [(2, half, thin, wide), (half, thin, wide), (half, thin, wide), (cols, 2, half, thin, wide)]
     semaphores = [pltpu.SemaphoreType.DMA((rows,))] * 2 + [pltpu.SemaphoreType.DMA((half,))] * 4
     steps = [1, half, half, 1, cols // 2, cols // 2]
@@ -504,7 +521,7 @@
     total = width * cols
     thick = trailing_t.shape[0] // rows
     tiled = width % BLOCK == 0 and total // rows % BLOCK == 0 and width // rows % (cols * MICRO) == 0 and thick % MICRO == 0
-    if tiled and rows % 2 == 0 and cols % 2 == 0 and rows // 2 + LATE < total // BLOCK and cols >= 4 and rows >= 4:
+    if tiled and rows % 2 == 0 and cols % 2 == 0 and rows // 2 + LATE < total // BLOCK and cols >= 4 and rows % 4 == 0 and BLOCK % (rows * MICRO) == 0 and width == 2 * BLOCK:
         return direct(panels_t, trailing_t, rows, cols)
     r_full, coef_block = plain(panels_t, trailing_t)
     rows_out = total // rows

time: 121 us -> 109 us (0.901)
  Pallas kernels: 117 us -> 105 us
    pallas_call x1, Pallas kernels: 117 us -> 105 us  [direct(): pl.pallas_call(lambda *refs: main_kernel(rows, cols, width, *refs), out_s...]
where the time goes in v3:
time: 109 us
  Pallas kernels  105 us (96%)
  local copies, waits for them, and re-layouts  3.65 us (3%)
    pallas_call x1, Pallas kernels, direct(): pl.pallas_call(lambda *refs: main_kernel(rows, cols, width, *refs), out_s...  105 us
    unnamed x6, local copies, waits for them, and re-layouts  3.65 us

profile of v3, /device:TPU:0, one launch (start us, length us, event | category | flops | bytes accessed | tf_op | source)
XLA Modules:
  0.0 109.3 jit_solution(6155577198594032375)
XLA Ops:
  0.6 0.0 copy-start
  0.6 1.1 %copy-done = f32[768,256]{1,0:T(8,128)S(1)} copy-done((f32[768,256]{1,0:T(8,128)S(1)}, f32[768,256]{1,0:T(8,128)}, u32[]{:S(2)}) %copy-start) | copy-done | bytes 786456
  1.8 0.0 copy-start.1
  1.8 0.9 copy-done.1
  2.7 105.0 %shard_map.41 = (f32[128,256]{1,0:T(8,128)S(1)}, f32[8,96,128]{2,1,0:T(8,128)S(1)}) custom-call(f32[256,256]{1,0:T(8,128)S(1)} %copy-done.1, f32[8,96,256]{2,1,0:T(8,128)S(1)} %bitcast.4), custom_call_target="tpu_custom_call" | custom-call | tf_op jit(solution)/shard_map/pallas_call | solution.py:490
  107.7 0.9 copy.4
  108.6 0.7 copy.6
Async XLA Ops:
  0.6 1.1 %copy-start = (f32[768,256]{1,0:T(8,128)S(1)}, f32[768,256]{1,0:T(8,128)}, u32[]{:S(2)}) copy-start(f32[768,256]{1,0:T(8,128)} %param.3) | copy-start | bytes 2359300
  1.8 0.9 copy-start.1

commit v4 on v3

--- a/solution.py
+++ b/solution.py
@@ -7,7 +7,7 @@
 
 BLOCK = 128
 MICRO = 8
-LATE = 1
+LATE = 0
 MESH = pl.DeviceIdType.MESH
 
 
@@ -101,11 +101,18 @@
         inverse_ref[here, :] = jnp.where(column < start, panel, 0.0)
         inverse_ref[here, here] = inverse
 
-        @pl.loop(k + 1, total // BLOCK)
+        def update(begin, size):
+            there = pl.ds(pl.multiple_of(begin * BLOCK, BLOCK), size)
+            work_ref[there, here] = jnp.zeros((size, BLOCK), jnp.float32)
+            work_ref[there, :] -= contract(work_ref[here, there], work_ref[here, :], 0, 0)
+
+        left = total // BLOCK - 1 - k
+        odd = lax.rem(left, 2)
+        pl.when(odd == 1)(lambda: update(k + 1, BLOCK))
+
+        @pl.loop(0, left // 2)
         def _(i):
-            there = pl.ds(pl.multiple_of(i * BLOCK, BLOCK), BLOCK)
-            work_ref[there, here] = jnp.zeros((BLOCK, BLOCK), jnp.float32)
-            work_ref[there, :] -= contract(work_ref[here, there], work_ref[here, :], 0, 0)
+            update(k + 1 + odd + 2 * i, 2 * BLOCK)
 
 
 def factor_kernel(gram_ref, upper_ref, inverse_ref, work_ref):
@@ -151,7 +158,7 @@
     return [(row, lax.rem(col + 2 * t, cols)) for t in range(1, cols // 2)] + [(row, mate)]
 
 
-def gather_columns(cols, pieces, ready, view, sems):
+def gather_columns(cols, pieces, ready, view, sems, early):
     line_send, line_recv, mate_send, mate_recv = sems
     row, col = lax.axis_index("row"), lax.axis_index("col")
     mate = col + 1 - 2 * lax.rem(col, 2)
@@ -180,11 +187,14 @@
         to_mate(source, col, s, 0)
         if s > 0:
             relay(s - 1)
-    relay(pieces - 1)
     for s in range(pieces):
+        if s == pieces - 1:
+            relay(s)
         for t in range(half):
             place = view(lax.rem(mate - 2 * t + cols, cols), s)
             remote(place, place, mate_send.at[s, t], mate_recv.at[s, t], row, mate).wait_recv()
+        if s == 0:
+            early()
     for copy in sent:
         copy.wait_send()
 
@@ -193,15 +203,15 @@
     return [pltpu.SemaphoreType.DMA((pieces, cols // 2))] * 4
 
 
-def gather_panel(cols, block_ref, panel_ref, sems):
+def gather_panel(cols, block_ref, panel_ref, sems, early):
     pieces = sems[0].shape[0]
     size = block_ref.shape[0] // pieces
 
     def part(s):
         return pl.ds(s * size, size)
 
-    gather_columns(cols, pieces, lambda s: block_ref.at[part(s)], lambda c, s: panel_ref.at[c, part(s)], sems)
     panel_ref[lax.axis_index("col")] = block_ref[...]
+    gather_columns(cols, pieces, lambda s: block_ref.at[part(s)], lambda c, s: panel_ref.at[c, part(s)], sems, early)
 
 
 class Reduction:
@@ -253,7 +263,8 @@
 class Gram:
     STAGES = 7
 
-    def __init__(self, rows, cols, width, panel_ref, buffers, sems):
+    def __init__(self, rows, cols, width, block_ref, panel_ref, buffers, sems):
+        self.block = block_ref
         self.rows, self.cols, self.width, self.panel = rows, cols, width, panel_ref
         self.buffers, self.sems = buffers, sems
         self.row, self.col = lax.axis_index("row"), lax.axis_index("col")
@@ -283,7 +294,7 @@
         if st == 0:
             if first is None:
                 strip = self.panel[0, own * BLOCK : (own + 1) * BLOCK, :]
-                right = self.panel[col]
+                right = self.block[...]
             else:
                 strip = self.panel[own, pl.ds(pl.multiple_of(col * (thin * self.rows), MICRO), thin * self.rows), :]
                 right = self.panel[first:last].reshape((last - first) * self.width, -1)
@@ -329,8 +340,11 @@
 
     def wave(self, w):
         for ch in range(len(self.chunks)):
-            if 0 <= w - ch < self.STAGES:
-                self.stage(ch, w - ch)
+            if 0 <= w - self.lag(ch) < self.STAGES:
+                self.stage(ch, w - self.lag(ch))
+
+    def lag(self, ch):
+        return ch + (ch == len(self.chunks) - 1)
 
     def place_chunk(self, ch, work_ref, add):
         own, first, last = self.chunks[ch]
@@ -410,8 +424,8 @@
     buffers = [refs[36 + 4 * i : 40 + 4 * i] for i in range(len(chunks))]
     row, col = lax.axis_index("row"), lax.axis_index("col")
     greet([(lax.rem(row + s, rows), col) for s in range(1, rows)] + column_peers(cols))
-    gather_panel(cols, block_ref, panel_ref, first)
-    gram = Gram(rows, cols, width, panel_ref, buffers, steps)
+    gram = Gram(rows, cols, width, block_ref, panel_ref, buffers, steps)
+    gather_panel(cols, block_ref, panel_ref, first, lambda: gram.wave(0))
     wide = Reduction(rows, cross_ref, pair_ref, line_ref, pairs, lines)
     total = work_ref.shape[0]
 
@@ -423,7 +437,6 @@
             cross_ref[r] = contract(trailing_ref[r], panel, 1, 1)
 
     ready = Gram.STAGES
-    gram.wave(0)
     work_ref[...] = jnp.zeros_like(work_ref)
     gram.wave(1)
     multiply(0, rows // 4)
@@ -436,15 +449,20 @@
     gram.wave(5)
     gram.wave(6)
     gram.place_chunk(0, work_ref, False)
+    wide.start(1, 2)
 
     def beside(k):
-        for w in range(ready, ready + len(chunks) - 1):
+        for w in range(ready, ready + len(chunks)):
             @pl.when(k == w - ready)
             def _(w=w):
                 gram.wave(w)
-                gram.place_chunk(w - ready + 1, work_ref, w > ready)
+                for ch in range(1, len(chunks)):
+                    if gram.lag(ch) + ready - 1 == w:
+                        gram.place_chunk(ch, work_ref, ch > 1)
                 if w == ready:
-                    wide.start(1, rows // 2 + 1)
+                    wide.start(2, 3)
+                if w == ready + 1:
+                    wide.start(3, rows // 2 + 1)
         for s in range(1, rows // 2):
             pl.when(k == s + LATE)(lambda s=s: wide.fold(s))
 
@@ -521,7 +539,7 @@
     total = width * cols
     thick = trailing_t.shape[0] // rows
     tiled = width % BLOCK == 0 and total // rows % BLOCK == 0 and width // rows % (cols * MICRO) == 0 and thick % MICRO == 0
-    if tiled and rows % 2 == 0 and cols % 2 == 0 and rows // 2 + LATE < total // BLOCK and cols >= 4 and rows % 4 == 0 and BLOCK % (rows * MICRO) == 0 and width == 2 * BLOCK:
+    if tiled and rows % 2 == 0 and cols % 2 == 0 and rows // 2 + LATE < total // BLOCK and cols >= 4 and rows % 4 == 0 and rows >= 8 and BLOCK % (rows * MICRO) == 0 and width == 2 * BLOCK:
         return direct(panels_t, trailing_t, rows, cols)
     r_full, coef_block = plain(panels_t, trailing_t)
     rows_out = total // rows

time: 109 us -> 104 us (0.954)
  Pallas kernels: 105 us -> 99.2 us
    pallas_call x1, Pallas kernels: 105 us -> 99.2 us  [direct(): pl.pallas_call(lambda *refs: main_kernel(rows, cols, width, *refs), out_s...]
where the time goes in v4:
time: 104 us; the launch traced here: 103 us
  Pallas kernels  99.2 us (95%)
  local copies, waits for them, and re-layouts  3.65 us (4%)
    pallas_call x1, Pallas kernels, direct(): pl.pallas_call(lambda *refs: main_kernel(rows, cols, width, *refs), out_s...  99.2 us
    unnamed x6, local copies, waits for them, and re-layouts  3.65 us

profile of v4, /device:TPU:0, one launch (start us, length us, event | category | flops | bytes accessed | tf_op | source)
XLA Modules:
  0.0 103.5 jit_solution(16643563766432553237)
XLA Ops:
  0.6 0.0 copy-start
  0.6 1.1 %copy-done = f32[768,256]{1,0:T(8,128)S(1)} copy-done((f32[768,256]{1,0:T(8,128)S(1)}, f32[768,256]{1,0:T(8,128)}, u32[]{:S(2)}) %copy-start) | copy-done | bytes 786456
  1.8 0.0 copy-start.1
  1.8 0.9 copy-done.1
  2.7 99.2 %shard_map.41 = (f32[128,256]{1,0:T(8,128)S(1)}, f32[8,96,128]{2,1,0:T(8,128)S(1)}) custom-call(f32[256,256]{1,0:T(8,128)S(1)} %copy-done.1, f32[8,96,256]{2,1,0:T(8,128)S(1)} %bitcast.4), custom_call_target="tpu_custom_call" | custom-call | tf_op jit(solution)/shard_map/pallas_call | solution.py:508
  101.9 0.9 copy.4
  102.8 0.7 copy.6
Async XLA Ops:
  0.6 1.1 %copy-start = (f32[768,256]{1,0:T(8,128)S(1)}, f32[768,256]{1,0:T(8,128)}, u32[]{:S(2)}) copy-start(f32[768,256]{1,0:T(8,128)} %param.3) | copy-start | bytes 2359300
  1.8 0.9 copy-start.1
